TPU v7x, 128 devices: a whole 4x4x4 slice. The times are simulated.
128 devices in a mesh: fsdp: 4 (over x_hi, core), ctx: 32 (over y, z, x_lo).
Axes of the slice: x: 4 (x_hi: 2, x_lo: 2; x = x_hi * 2 + x_lo), y: 4, z: 4, core: 2. Of those that a mesh axis runs over, the one named last changes fastest.
Arguments:
- query_branch: bfloat16 [4, 8192, 4096], P('fsdp', 'ctx'), may hold values from -6 to 6
- key_branch: bfloat16 [4, 8192, 4096], P('fsdp', 'ctx'), may hold values from -6 to 6
- value_branch: bfloat16 [4, 8192, 4096], P('fsdp', 'ctx'), may hold values from -6 to 6
- cotangent: bfloat16 [4, 8192, 4096], P('fsdp', 'ctx'), may hold values from -6 to 6
- quantized_weight_codes: int32 [4096, 4096], P('ctx', 'fsdp'), may hold values from 0 to 15
- scale_code_bytes: int32 [4096, 64], P('ctx', 'fsdp'), may hold values from 0 to 255
- row_scale_second: float32 [4096], P('ctx'), may hold values from 0.01 to 0.1
- filters: bfloat16 [256, 128], replicated, may hold values from -0.5 to 0.5
- channel_skip_weight: float32 [4096], replicated, may hold values from -6 to 6
- adapter_down_weight: bfloat16 [4096, 64], P('ctx'), may hold values from -0.09375 to 0.09375
- adapter_up_weight: bfloat16 [64, 4096], P(None, 'fsdp'), may hold values from -0.75 to 0.75
Outputs:
- output: bfloat16 [4, 8192, 4096], P('fsdp', 'ctx')
- grad_query: bfloat16 [4, 8192, 4096], P('fsdp', 'ctx')
- grad_key: bfloat16 [4, 8192, 4096], P('fsdp', 'ctx')
- grad_value: bfloat16 [4, 8192, 4096], P('fsdp', 'ctx')
- grad_down: bfloat16 [4096, 64], P('ctx')
- grad_up: bfloat16 [64, 4096], P(None, 'fsdp')
All inputs are finite; a program needn't handle non-finite values.
Results may differ from a plain program's by a relative error of at most 0.0067.
Values may be sent and summed in bfloat16 or wider, within the bound.
No kernel may reach another device: no remote copies, remote signals or barrier semaphores. Data moves between devices by JAX's collectives and lax.ppermute only.
A program may use at most 256 MiB of HBM per device.

v0:
```python
import math
import jax
import jax.numpy as jnp
from jax import lax
from jax.sharding import PartitionSpec as P

QBLOCK = 64
normal_levels = (
    -1.0,
    -0.6961928009986877,
    -0.5250730514526367,
    -0.39491748809814453,
    -0.28444138169288635,
    -0.18477343022823334,
    -0.09105003625154495,
    0.0,
    0.07958029955625534,
    0.16093020141124725,
    0.24611230194568634,
    0.33791524171829224,
    0.44070982933044434,
    0.5626170039176941,
    0.7229568362236023,
    1.0,
)
adapter_scale = 0.25


def from_behind(shard, axis, by):
    count = lax.axis_size(axis)
    pairs = [(i, i + by) for i in range(count) if 0 <= i + by < count]
    return lax.ppermute(shard, axis, pairs)


def dequantize(quantized_weight_codes, scale_code_bytes, row_scale_second):
    levels = jnp.zeros(quantized_weight_codes.shape, jnp.float32)
    for number in range(16):
        levels = jnp.where(quantized_weight_codes == number, normal_levels[number], levels)
    absmax = row_scale_second[:, None] * (scale_code_bytes.astype(jnp.float32) + 1.0) / 256.0
    absmax = jnp.repeat(absmax, QBLOCK, axis=1)
    return (levels * absmax).astype(jnp.bfloat16)


def toeplitz(filter_taps, filter_len):
    groups = filter_taps.shape[0]
    padded = jnp.concatenate([filter_taps, jnp.zeros((groups, filter_len), filter_taps.dtype)], 1)
    repeated = jnp.tile(padded, (1, filter_len))[:, : filter_len * (2 * filter_len - 1)]
    return repeated.reshape(groups, filter_len, 2 * filter_len - 1)


def block_conv(extended, toep, filter_len):
    row_count = extended.shape[0] - (filter_len - 1)
    blocks = row_count // filter_len
    current = extended[:row_count].reshape(blocks, filter_len, -1)
    following = jnp.concatenate(
        [extended[filter_len:], jnp.zeros((1, extended.shape[1]), extended.dtype)], 0
    )
    following = following.reshape(blocks, filter_len, -1)[:, : filter_len - 1]
    windows = jnp.concatenate([current, following], 1)
    windows = windows.reshape(blocks, 2 * filter_len - 1, toep.shape[0], -1)
    result = jnp.einsum("gts,bsgk->btgk", toep, windows, preferred_element_type=jnp.float32)
    return result.reshape(row_count, -1)


def local(
    query_branch,
    key_branch,
    value_branch,
    cotangent,
    quantized_weight_codes,
    scale_code_bytes,
    row_scale_second,
    filters,
    channel_skip_weight,
    adapter_down_weight,
    adapter_up_weight,
):
    filter_len = filters.shape[1]
    queries = query_branch[0]
    output_gradient = cotangent[0]
    row_count, channels = queries.shape
    token_count = query_branch.shape[0] * row_count * lax.axis_size("ctx") * lax.axis_size("fsdp")
    multiplier = adapter_scale / math.sqrt(token_count)
    query_float = queries.astype(jnp.float32)
    key_float = key_branch[0].astype(jnp.float32)
    value_float = value_branch[0].astype(jnp.float32)
    mixed = (key_float * value_float).astype(jnp.bfloat16)
    before = from_behind(mixed[row_count - (filter_len - 1) :], "ctx", 1)
    ahead_toep = toeplitz(jnp.flip(filters, 1), filter_len)
    back_toep = toeplitz(filters, filter_len)
    gated = block_conv(
        jnp.concatenate([before, mixed], 0), ahead_toep, filter_len
    ) + channel_skip_weight * mixed.astype(jnp.float32)
    gated_signal = (query_float * gated).astype(jnp.bfloat16)
    local_piece = dequantize(quantized_weight_codes, scale_code_bytes, row_scale_second)
    local_rows, up_complete = (
        lax.all_gather(local_piece, "fsdp", axis=1, tiled=True),
        lax.all_gather(adapter_up_weight, "fsdp", axis=1, tiled=True),
    )
    backward_up_term = jnp.einsum(
        "td,rd->tr", output_gradient, up_complete, preferred_element_type=jnp.float32
    ).astype(jnp.bfloat16)
    weight_rows = lax.all_gather(local_rows, "ctx", axis=0, tiled=True)
    rank_rows = lax.all_gather(adapter_down_weight, "ctx", axis=0, tiled=True)
    output_total = jnp.dot(gated_signal, weight_rows, preferred_element_type=jnp.float32)
    down_sum = jnp.dot(gated_signal, rank_rows, preferred_element_type=jnp.float32)
    elementwise_product = jnp.einsum(
        "td,cd->tc", output_gradient, weight_rows, preferred_element_type=jnp.float32
    )
    elementwise_product = elementwise_product + adapter_scale * jnp.einsum(
        "tr,cr->tc", backward_up_term, rank_rows, preferred_element_type=jnp.float32
    )
    down_projection = down_sum.astype(jnp.bfloat16)
    output = (
        output_total
        + adapter_scale * jnp.dot(down_projection, up_complete, preferred_element_type=jnp.float32)
    ).astype(jnp.bfloat16)
    grad_query = (elementwise_product * gated).astype(jnp.bfloat16)
    grad_gated = (elementwise_product * query_float).astype(jnp.bfloat16)
    leading = jnp.concatenate(
        [jnp.zeros((filter_len, channels), jnp.bfloat16), grad_gated[: filter_len - 1]], 0
    )
    spill = block_conv(leading, back_toep, filter_len)
    arrived = from_behind(spill[1:], "ctx", -1)
    tail_rows = jnp.concatenate(
        [grad_gated, jnp.zeros((filter_len - 1, channels), jnp.bfloat16)], 0
    )
    local_grad = block_conv(tail_rows, back_toep, filter_len)
    local_grad = local_grad + jnp.concatenate(
        [jnp.zeros((row_count - filter_len + 1, channels), jnp.float32), arrived], 0
    )
    grad_mixed = local_grad + channel_skip_weight * grad_gated.astype(jnp.float32)
    grad_key = (grad_mixed * value_float).astype(jnp.bfloat16)
    grad_value = (grad_mixed * key_float).astype(jnp.bfloat16)
    term_down = multiplier * jnp.einsum(
        "tc,tr->cr", gated_signal, backward_up_term, preferred_element_type=jnp.float32
    )
    term_up = multiplier * jnp.einsum(
        "tr,td->rd", down_projection, output_gradient, preferred_element_type=jnp.float32
    )
    total_down = lax.psum(term_down, "fsdp")
    grad_down = lax.psum_scatter(total_down, "ctx", scatter_dimension=0, tiled=True)
    total_up = lax.psum(term_up, "ctx")
    grad_up = lax.psum_scatter(total_up, "fsdp", scatter_dimension=1, tiled=True)
    return (
        output[None],
        grad_query[None],
        grad_key[None],
        grad_value[None],
        grad_down.astype(jnp.bfloat16),
        grad_up.astype(jnp.bfloat16),
    )


def solution(mesh):
    return jax.shard_map(
        local,
        mesh=mesh,
        in_specs=(
            P("fsdp", "ctx", None),
            P("fsdp", "ctx", None),
            P("fsdp", "ctx", None),
            P("fsdp", "ctx", None),
            P("ctx", "fsdp"),
            P("ctx", "fsdp"),
            P("ctx"),
            P(),
            P(),
            P("ctx", None),
            P(None, "fsdp"),
        ),
        out_specs=(
            P("fsdp", "ctx", None),
            P("fsdp", "ctx", None),
            P("fsdp", "ctx", None),
            P("fsdp", "ctx", None),
            P("ctx", None),
            P(None, "fsdp"),
        ),
        check_vma=False,
    )
```

profile of v0, /device:TPU:1, one launch (start us, length us, event | category | flops | bytes accessed | tf_op | source)
XLA Modules:
  0.0 1086.2 jit_solution(9586040226539737358)
XLA Ops:
  7.2 0.0 all-gather.3.cloned.1.call-start
  7.2 1.4 copy.29
  8.6 0.7 multiply_multiply_fusion
  9.3 1.3 fusion.40
  10.6 0.0 all-gather.5.cloned.1.call-start
  10.7 24.5 %all-gather.3.cloned.1.call-done = bf16[128,4096]{0,1:T(8,128)(2,1)} async-done(((bf16[128,1024]{0,1:T(8,128)(2,1)}), bf16[128,4096]{0,1:T(8,128)(2,1)}) %all-gather.3.cloned.1.call-update) | async-done | bytes 1048592 | tf_op jit(solution)/shard_map/all_gather | solution.py:97
  35.2 0.0 reduce-scatter.5.cloned.1.call-start
  35.2 3.0 fusion.11
  38.3 1.5 slice.49
  39.8 3.2 collective-permute-start
  42.9 1.8 slice.50
  44.8 0.2 rev.4
  45.0 1.3 tile.20
  46.3 41.7 %copy.62 = bf16[32,8,128,256]{3,1,2,0:T(8,128)(2,1)S(1)} copy(bf16[32,8,128,256]{3,2,1,0:T(8,128)(2,1)S(1)} %bitcast.101) | data formatting | bytes 33554432
  88.0 6.6 slice.54
  94.6 56.8 %reshape.84 = bf16[256,128,255,1]{2,1,0,3:T(8,128)(2,1)} reshape(bf16[256,32640]{1,0:T(8,128)(2,1)} %slice.54) | data formatting | bytes 33423360 | tf_op jit(solution)/shard_map/reshape | solution.py:48
  151.3 56.7 %reshape.76 = bf16[256,128,255]{2,1,0:T(8,128)(2,1)} reshape(bf16[256,32640]{1,0:T(8,128)(2,1)} %slice.54) | data formatting | bytes 33423360 | tf_op jit(solution)/shard_map/reshape | solution.py:48
  208.1 1.3 tile.8
  209.3 41.7 %copy.60 = bf16[32,8,128,256]{3,1,2,0:T(8,128)(2,1)S(1)} copy(bf16[32,8,128,256]{3,2,1,0:T(8,128)(2,1)S(1)} %bitcast.102) | data formatting | bytes 33554432
  251.0 6.6 slice.52
  257.6 56.8 %reshape.83 = bf16[256,128,255,1]{2,1,0,3:T(8,128)(2,1)} reshape(bf16[256,32640]{1,0:T(8,128)(2,1)} %slice.52) | data formatting | bytes 33423360 | tf_op jit(solution)/shard_map/reshape | solution.py:48
  314.4 3.2 concatenate.45
  317.6 4.2 copy.57
  321.8 12.4 %all_gather.15 = bf16[64,4096]{1,0:T(8,128)(2,1)S(1)} all-gather(bf16[64,1024]{1,0:T(8,128)(2,1)S(1)} %copy-done.11), channel_id=1, replica_groups=mesh['fsdp'=4,'ctx'=32] {'fsdp'}, dimensions={1}, use_global_device_ids=true | all-gather | bytes 655360 | tf_op jit(solution)/shard_map/all_gather | solution.py:98
  334.1 80.4 %all_gather.14 = bf16[4096,64]{0,1:T(8,128)(2,1)S(1)} all-gather(bf16[128,64]{0,1:T(8,128)(2,1)S(1)} %copy-done.13), channel_id=1, replica_groups=mesh['fsdp'=4,'ctx'=32] {'ctx'}, dimensions={0}, use_global_device_ids=true | all-gather | bytes 540672 | tf_op jit(solution)/shard_map/all_gather | solution.py:104
  414.6 0.8 fusion.36
  415.3 2.9 pad_maximum_fusion
  418.2 4.1 copy.23
  422.3 4.0 concatenate.44
  426.3 3.4 copy.25
  429.7 9.5 fusion.19
  439.2 2.2 copy.27
  441.3 2.2 copy.73
  443.6 5.7 copy.28
  449.2 329.5 %all-gather.5.cloned.1.call-done = bf16[4096,4096]{0,1:T(8,128)(2,1)} async-done(((bf16[128,4096]{0,1:T(8,128)(2,1)}), bf16[4096,4096]{0,1:T(8,128)(2,1)}) %all-gather.5.cloned.1.call-update) | async-done | bytes 33554448 | tf_op jit(solution)/shard_map/all_gather | solution.py:103
  778.8 17.2 %convolution_bitcast_fusion = f32[256,4096]{1,0:T(8,128)} fusion(bf16[4096,4096]{0,1:T(8,128)(2,1)} %all-gather.5.cloned.1.call-done, bf16[1,256,4096]{2,1,0:T(8,128)(2,1)S(1)} %copy-done), kind=kOutput, calls=%fused_computation.4 | convolution fusion | flops 8589934592 | bytes 39845888 | tf_op jit(solution)/shard_map/td,cd->tc/dot_general | solution.py:107
  796.0 6.7 fusion.29
  802.7 1.3 copy-done.6
  804.0 0.8 convolution_convert_fusion
  804.8 1.5 convolution_multiply_fusion.3
  806.2 0.3 reduce-scatter.3.cloned.1.call-start
  806.5 2.3 fusion.39
  808.9 2.3 copy.59
  811.2 2.8 concatenate.56.clone
  814.0 12.6 %convolution_bitcast_fusion.1 = f32[1,128,256,16]{1,3,2,0:T(8,128)} fusion(bf16[255,256,16]{0,2,1:T(8,128)(2,1)} %bitcast.111, bf16[256,128,255]{2,1,0:T(8,128)(2,1)} %reshape.76), kind=kOutput, calls=%fused_computation.45 | convolution fusion | flops 267386880 | bytes 20897792 | tf_op jit(solution)/shard_map/gts,bsgk->btgk/dot_general | solution.py:61
  826.6 3.7 slice.57
  830.3 3.0 copy.52
  833.2 1.3 collective-permute-start.1
  834.5 3.1 convolution_multiply_fusion.2
  837.6 17.7 %fusion.43 = f32[256,4096]{1,0:T(8,128)} fusion(bf16[256,4096]{1,0:T(8,128)(2,1)} %copy-done.6, bf16[4096,4096]{0,1:T(8,128)(2,1)} %all-gather.5.cloned.1.call-done), kind=kOutput, calls=%fused_computation.55 | convolution fusion | flops 8589934592 | bytes 39845888 | tf_op jit(solution)/shard_map/dot_general | solution.py:105
  855.3 4.1 copy.46
  859.4 4.0 concatenate.49
  863.3 3.3 copy.48
  866.7 0.2 pad_slice_fusion
  866.9 1.5 concatenate.51
  868.3 4.2 copy.58
  872.5 9.9 fusion.24
  882.4 2.2 copy.50
  884.6 2.3 copy.72
  886.9 5.7 copy.53
  892.5 4.4 fusion.7
  896.9 6.5 fusion.30
  903.4 135.5 %all-reduce.8 = bf16[64,1024]{1,0:T(8,128)(2,1)} all-reduce(f32[64,1024]{1,0:T(8,128)} %reduce-scatter.5.cloned.1.call-done), channel_id=1, replica_groups=mesh['fsdp'=4,'ctx'=32] {'ctx'}, use_global_device_ids=true, to_apply=%region_2.3 | all-reduce | flops 65536 | bytes 393216 | tf_op jit(solution)/shard_map/psum | solution.py:143
  1038.9 40.4 %psum.16 = bf16[128,64]{0,1:T(8,128)(2,1)} all-reduce(f32[128,64]{0,1:T(8,128)} %reduce-scatter.3.cloned.1.call-done), channel_id=1, replica_groups=mesh['fsdp'=4,'ctx'=32] {'fsdp'}, use_global_device_ids=true, to_apply=%region_0.1 | all-reduce | flops 8192 | bytes 49152 | tf_op jit(solution)/shard_map/psum | solution.py:141
  (39 shorter events, 0.2 us)
Async XLA Ops:
  7.2 407.4 %copy-start = (bf16[1,256,4096]{2,1,0:T(8,128)(2,1)S(1)}, bf16[1,256,4096]{2,1,0:T(8,128)(2,1)}, u32[]{:S(2)}) copy-start(bf16[1,256,4096]{2,1,0:T(8,128)(2,1)} %param.14) | copy-start | bytes 6291460
  7.2 28.0 %all-gather.3.cloned.1.call-start = ((), (), s32[]{:S(2)}) async-start(), calls=%async_computation.2 | async-start | bytes 1310720 | tf_op jit(solution)/shard_map/all_gather | solution.py:97
  10.6 768.1 %all-gather.5.cloned.1.call-start = ((), (), s32[]{:S(2)}) async-start(), calls=%async_computation.3 | async-start | bytes 34603008 | tf_op jit(solution)/shard_map/all_gather | solution.py:103
  35.2 868.2 %reduce-scatter.5.cloned.1.call-start = ((), (), s32[]{:S(2)}) async-start(), calls=%async_computation.5 | async-start | bytes 1310720 | tf_op jit(solution)/shard_map/reduce_scatter | solution.py:144
  38.2 4.7 copy-start.3
  38.2 6.5 copy-start.10
  39.8 375.6 %collective-permute-start = (bf16[127,4096]{1,0:T(8,128)(2,1)}, bf16[127,4096]{1,0:T(8,128)(2,1)}, u32[]{:S(2)}, u32[]{:S(2)}) collective-permute-start(bf16[127,4096]{1,0:T(8,128)(2,1)} %slice.49), channel_id=1, source_target_pairs={{0,1},{1,2},{2,3},{3,4},{4,5},{5,6},{6,7},{7,8},{8,9},{9,10},{10,1... | collective-permute-start | bytes 3121160 | tf_op jit(solution)/shard_map/ppermute | solution.py:32
  314.4 7.4 copy-start.11
  314.4 19.7 %copy-start.13 = (bf16[128,64]{0,1:T(8,128)(2,1)S(1)}, bf16[128,64]{0,1:T(8,128)(2,1)}, u32[]{:S(2)}) copy-start(bf16[128,64]{0,1:T(8,128)(2,1)} %param.20) | copy-start | bytes 49156
  321.8 93.6 %copy-start.4 = (bf16[256,4096]{1,0:T(8,128)(2,1)S(1)}, bf16[256,4096]{1,0:T(8,128)(2,1)}, u32[]{:S(2)}) copy-start(bf16[256,4096]{1,0:T(8,128)(2,1)} %copy-done.3) | copy-start | bytes 6291460
  426.3 3.4 copy-start.7
  449.2 346.7 %copy-start.12 = (f32[4096]{0:T(1024)S(1)}, f32[4096]{0:T(1024)}, u32[]{:S(2)}) copy-start(f32[4096]{0:T(1024)} %param.19) | copy-start | bytes 49156
  778.8 17.2 %copy-start.5 = (bf16[256,4096]{1,0:T(8,128)(2,1)S(1)}, bf16[256,4096]{1,0:T(8,128)(2,1)}, u32[]{:S(2)}) copy-start(bf16[256,4096]{1,0:T(8,128)(2,1)} %copy-done.3) | copy-start | bytes 6291460
  778.8 17.2 %copy-start.9 = (f32[256,4096]{1,0:T(8,128)S(1)}, f32[256,4096]{1,0:T(8,128)}, u32[]{:S(2)}) copy-start(f32[256,4096]{1,0:T(8,128)} %copy.28) | copy-start | bytes 12582916
  802.7 1.3 copy-start.6
  802.7 3.8 copy-start.14
  806.2 232.7 %reduce-scatter.3.cloned.1.call-start = ((), (), s32[]{:S(2)}) async-start(), calls=%async_computation.4 | async-start | bytes 1081344 | tf_op jit(solution)/shard_map/reduce_scatter | solution.py:142
  833.2 63.7 %collective-permute-start.1 = (f32[127,4096]{1,0:T(8,128)}, f32[127,4096]{1,0:T(8,128)}, u32[]{:S(2)}, u32[]{:S(2)}) collective-permute-start(f32[127,4096]{1,0:T(8,128)} %copy.52), channel_id=1, source_target_pairs={{1,0},{2,1},{3,2},{4,3},{5,4},{6,5},{7,6},{8,7},{9,8},{10,9},{11,1... | collective-permute-start | bytes 6242312 | tf_op jit(solution)/shard_map/ppermute | solution.py:32
  863.3 3.3 copy-start.1
  892.5 4.4 copy-start.2
  892.5 4.4 copy-start.8
Sparse Core Ops, SparseCore 0:
  10.8 24.3 all-gather.2
  36.7 742.0 all-gather.4
  806.4 30.7 reduce-scatter.4
  839.4 139.4 reduce-scatter.2
where the time goes:
time: 1100 us; the launch traced here: 1090 us
  waiting for transfers between devices  354 us (32%)
  local copies, waits for them, and re-layouts  344 us (31%)
  blocking collectives  269 us (24%)
  matrix products  84 us (8%)
  other arithmetic  16.8 us (2%)
  between operations  14.3 us (1%)
    all_gather x1, waiting for transfers between devices, local(): weight_rows = lax.all_gather(local_rows, 'ctx', axis=0, tiled=True)  330 us
    reshape x3, local copies, waits for them, and re-layouts, toeplitz(): return repeated.reshape(groups, filter_len, 2 * filter_len - 1)  170 us
    psum x1, blocking collectives, local(): total_up = lax.psum(term_up, 'ctx')  135 us
    unnamed x38, local copies, waits for them, and re-layouts  101 us
    all_gather x1, blocking collectives, local(): rank_rows = lax.all_gather(adapter_down_weight, 'ctx', axis=0, tiled=True)  80.4 us
    psum x1, blocking collectives, local(): total_down = lax.psum(term_down, 'fsdp')  40.4 us
    dot_general x3, matrix products, block_conv(): jnp.einsum('gts,bsgk->btgk', toep, windows, preferred_element_type=jnp.fl...  32 us
    all_gather x1, waiting for transfers between devices, local(): lax.all_gather(local_piece, 'fsdp', axis=1, tiled=True)  24.5 us
  transfers between devices with their start and end apart: 6, of which 2 were waited for; matrix products, arithmetic and copies ran while one was open for 38% of the time, Pallas kernels for 0%

commit v1 on v0

--- a/solution.py
+++ b/solution.py
@@ -3,6 +3,7 @@
 import jax.numpy as jnp
 from jax import lax
 from jax.sharding import PartitionSpec as P
+from jax.lax import all_to_all, psum
 
 QBLOCK = 64
 normal_levels = (
@@ -101,7 +102,15 @@
         "td,rd->tr", output_gradient, up_complete, preferred_element_type=jnp.float32
     ).astype(jnp.bfloat16)
     weight_rows = lax.all_gather(local_rows, "ctx", axis=0, tiled=True)
-    rank_rows = lax.all_gather(adapter_down_weight, "ctx", axis=0, tiled=True)
+    rank_rows = jnp.concatenate(
+        all_to_all(
+            jnp.stack([adapter_down_weight for _ in range(psum(1, axis_name="ctx"))], axis=0),
+            axis_name="ctx",
+            split_axis=0,
+            concat_axis=0,
+        ),
+        axis=0,
+    )
     output_total = jnp.dot(gated_signal, weight_rows, preferred_element_type=jnp.float32)
     down_sum = jnp.dot(gated_signal, rank_rows, preferred_element_type=jnp.float32)
     elementwise_product = jnp.einsum(

time: 1100 us -> 1190 us (1.082); the launches traced: 1090 us -> 1190 us
  waiting for transfers between devices: 354 us -> 500 us
  blocking collectives: 269 us -> 199 us
  local copies, waits for them, and re-layouts: 344 us -> 358 us
    all_gather x1, waiting for transfers between devices: 330 us -> 420 us  [local(): weight_rows = lax.all_gather(local_rows, 'ctx', axis=0, tiled=True)]
    all_gather x1 -> x0, blocking collectives: 80.4 us -> none  [local(): rank_rows = lax.all_gather(adapter_down_weight, 'ctx', axis=0, tiled=True)]
    reduce_scatter x1, waiting for transfers between devices: 0.01 us -> 79.7 us  [local(): lax.psum_scatter(total_down, 'ctx', scatter_dimension=0, tiled=True)]
    all_gather x1, waiting for transfers between devices: 24.5 us -> 0.02 us  [local(): lax.all_gather(local_piece, 'fsdp', axis=1, tiled=True)]
    psum x1, blocking collectives: 135 us -> 148 us  [local(): total_up = lax.psum(term_up, 'ctx')]
    reshape x2 -> x4, local copies, waits for them, and re-layouts: 11.3 us -> 23.5 us  [block_conv(): return result.reshape(row_count, -1)]
    unnamed x38 -> x48, local copies, waits for them, and re-layouts: 101 us -> 101 us
  transfers between devices with their start and end apart: 6 -> 7, of which waited for: 2 -> 2; matrix products, arithmetic and copies ran while one was open for 38% -> 34% of each run, Pallas kernels for 0% -> 0%
where the time goes in v1:
time: 1190 us
  waiting for transfers between devices  500 us (42%)
  local copies, waits for them, and re-layouts  358 us (30%)
  blocking collectives  199 us (17%)
  matrix products  87.3 us (7%)
  starting transfers between devices  15.5 us (1%)
  other arithmetic  15.4 us (1%)
  between operations  14.3 us (1%)
    all_gather x1, waiting for transfers between devices, local(): weight_rows = lax.all_gather(local_rows, 'ctx', axis=0, tiled=True)  420 us
    reshape x3, local copies, waits for them, and re-layouts, toeplitz(): return repeated.reshape(groups, filter_len, 2 * filter_len - 1)  170 us
    psum x1, blocking collectives, local(): total_up = lax.psum(term_up, 'ctx')  148 us
    unnamed x48, local copies, waits for them, and re-layouts  101 us
    reduce_scatter x1, waiting for transfers between devices, local(): lax.psum_scatter(total_down, 'ctx', scatter_dimension=0, tiled=True)  79.7 us
    psum x1, blocking collectives, local(): total_down = lax.psum(term_down, 'fsdp')  38.1 us
    dot_general x3, matrix products, block_conv(): jnp.einsum('gts,bsgk->btgk', toep, windows, preferred_element_type=jnp.fl...  31.2 us
  transfers between devices with their start and end apart: 7, of which 2 were waited for; matrix products, arithmetic and copies ran while one was open for 34% of the time, Pallas kernels for 0%

profile of v1, /device:TPU:1, one launch (start us, length us, event | category | flops | bytes accessed | tf_op | source)
XLA Modules:
  0.0 1190.1 jit_solution(15048625238681174294)
XLA Ops:
  7.3 3.2 fusion.17
  10.4 1.3 copy-done.2
  11.8 1.3 slice.49
  13.0 5.0 collective-permute-start
  18.3 1.3 fusion.55
  19.6 0.9 stack.2
  20.6 8.0 all-to-all-start
  28.5 0.3 reduce-scatter.5.cloned.1.call-start
  28.9 3.4 slice.50
  32.3 0.2 rev.4
  32.5 1.3 tile.8
  33.8 41.7 %copy.132 = bf16[32,8,128,256]{3,1,2,0:T(8,128)(2,1)S(1)} copy(bf16[32,8,128,256]{3,2,1,0:T(8,128)(2,1)S(1)} %bitcast.141) | data formatting | bytes 33554432
  75.5 6.5 slice.52
  82.1 56.7 %reshape.99 = bf16[256,128,255,1]{2,1,0,3:T(8,128)(2,1)} reshape(bf16[256,32640]{1,0:T(8,128)(2,1)} %slice.52) | data formatting | bytes 33423360 | tf_op jit(solution)/shard_map/reshape | solution.py:49
  138.8 3.1 concatenate.45
  141.9 4.1 copy.128
  146.1 3.2 pad_maximum_fusion
  149.3 4.1 copy.91
  153.3 4.0 concatenate.44
  157.3 3.3 copy.93
  160.6 9.5 fusion.26
  170.1 4.2 copy.95
  174.3 6.5 reshape.89
  180.8 5.6 copy.114
  186.4 5.4 fusion.46
  191.9 1.5 convolution_multiply_fusion.3
  193.5 0.7 all-gather.5.cloned.1.call-update
  194.1 0.6 reduce-scatter.3.cloned.1.call-start
  194.7 1.3 tile.20
  196.0 41.7 %copy.134 = bf16[32,8,128,256]{3,1,2,0:T(8,128)(2,1)S(1)} copy(bf16[32,8,128,256]{3,2,1,0:T(8,128)(2,1)S(1)} %bitcast.142) | data formatting | bytes 33554432
  237.7 6.6 slice.54
  244.3 56.7 %reshape.100 = bf16[256,128,255,1]{2,1,0,3:T(8,128)(2,1)} reshape(bf16[256,32640]{1,0:T(8,128)(2,1)} %slice.54) | data formatting | bytes 33423360 | tf_op jit(solution)/shard_map/reshape | solution.py:49
  301.1 56.8 %reshape.92 = bf16[256,128,255]{2,1,0:T(8,128)(2,1)} reshape(bf16[256,32640]{1,0:T(8,128)(2,1)} %slice.54) | data formatting | bytes 33423360 | tf_op jit(solution)/shard_map/reshape | solution.py:49
  357.8 13.1 %all_gather.11 = bf16[64,4096]{1,0:T(8,128)(2,1)S(1)} all-gather(bf16[64,1024]{1,0:T(8,128)(2,1)S(1)} %copy-done.15), channel_id=1, replica_groups=mesh['fsdp'=4,'ctx'=32] {'fsdp'}, dimensions={1}, use_global_device_ids=true | all-gather | bytes 655360 | tf_op jit(solution)/shard_map/all_gather | solution.py:99
  370.9 0.8 fusion.49
  371.6 4.5 copy.155
  376.1 5.7 copy.96
  381.9 148.0 %all-reduce.8 = bf16[64,1024]{1,0:T(8,128)(2,1)} all-reduce(f32[64,1024]{1,0:T(8,128)} %reduce-scatter.5.cloned.1.call-done), channel_id=1, replica_groups=mesh['fsdp'=4,'ctx'=32] {'ctx'}, use_global_device_ids=true, to_apply=%region_2.3 | all-reduce | flops 65536 | bytes 393216 | tf_op jit(solution)/shard_map/psum | solution.py:152
  529.8 419.9 %all-gather.5.cloned.1.call-done = bf16[4096,4096]{0,1:T(8,128)(2,1)} async-done(((bf16[128,4096]{0,1:T(8,128)(2,1)}), bf16[4096,4096]{0,1:T(8,128)(2,1)}) %all-gather.5.cloned.1.call-update) | async-done | bytes 33554448 | tf_op jit(solution)/shard_map/all_gather | solution.py:104
  949.8 17.2 %convolution_bitcast_fusion = f32[256,4096]{1,0:T(8,128)} fusion(bf16[4096,4096]{0,1:T(8,128)(2,1)} %all-gather.5.cloned.1.call-done, bf16[1,256,4096]{2,1,0:T(8,128)(2,1)S(1)} %copy-done), kind=kOutput, calls=%fused_computation.4 | convolution fusion | flops 8589934592 | bytes 39845888 | tf_op jit(solution)/shard_map/td,cd->tc/dot_general | solution.py:116
  967.0 6.2 fusion.36
  973.2 1.2 fusion.52
  974.4 2.3 copy.130
  976.7 2.8 concatenate.56.clone
  979.5 12.2 %convolution_bitcast_fusion.1 = f32[1,128,256,16]{1,3,2,0:T(8,128)} fusion(bf16[255,256,16]{0,2,1:T(8,128)(2,1)} %bitcast.151, bf16[256,128,255]{2,1,0:T(8,128)(2,1)} %reshape.92), kind=kOutput, calls=%fused_computation.54 | convolution fusion | flops 267386880 | bytes 20897792 | tf_op jit(solution)/shard_map/gts,bsgk->btgk/dot_general | solution.py:62
  991.8 3.5 slice.57
  995.3 3.0 copy.123
  998.2 1.5 collective-permute-start.1
  999.7 3.1 convolution_multiply_fusion.2
  1002.8 17.6 %fusion.62 = f32[256,4096]{1,0:T(8,128)} fusion(bf16[256,4096]{1,0:T(8,128)(2,1)} %get-tuple-element.9, bf16[4096,4096]{0,1:T(8,128)(2,1)} %all-gather.5.cloned.1.call-done), kind=kOutput, calls=%fused_computation.68 | convolution fusion | flops 8589934592 | bytes 39845888 | tf_op jit(solution)/shard_map/dot_general | solution.py:114
  1020.5 2.4 copy.117
  1022.9 4.0 concatenate.49
  1026.9 3.2 copy.119
  1030.0 0.2 pad_slice_fusion
  1030.2 1.5 concatenate.51
  1031.7 3.2 copy.129
  1034.9 9.5 fusion.31
  1044.4 2.2 copy.121
  1046.6 2.3 copy.154
  1048.9 5.6 copy.124
  1054.5 4.4 fusion.12
  1059.0 6.6 fusion.38
  1065.5 79.7 %reduce-scatter.3.cloned.1.call-done = f32[128,64]{0,1:T(8,128)} async-done(((f32[4096,64]{0,1:T(8,128)}), f32[128,64]{0,1:T(8,128)}) %reduce-scatter.3.cloned.1.call-update) | async-done | bytes 32784 | tf_op jit(solution)/shard_map/reduce_scatter | solution.py:151
  1145.2 38.1 %psum.16 = bf16[128,64]{0,1:T(8,128)(2,1)} all-reduce(f32[128,64]{0,1:T(8,128)} %reduce-scatter.3.cloned.1.call-done), channel_id=1, replica_groups=mesh['fsdp'=4,'ctx'=32] {'fsdp'}, use_global_device_ids=true, to_apply=%region_0.1 | all-reduce | flops 8192 | bytes 49152 | tf_op jit(solution)/shard_map/psum | solution.py:150
  (53 shorter events, 0.5 us)
Async XLA Ops:
  7.2 184.7 %copy-start = (bf16[1,256,4096]{2,1,0:T(8,128)(2,1)S(1)}, bf16[1,256,4096]{2,1,0:T(8,128)(2,1)}, u32[]{:S(2)}) copy-start(bf16[1,256,4096]{2,1,0:T(8,128)(2,1)} %param.14) | copy-start | bytes 6291460
  7.2 10.9 copy-start.12
  7.2 11.1 copy-start.17
  7.2 11.1 copy-start.19
  7.2 12.4 %copy-start.16 = (bf16[128,64]{0,1:T(8,128)(2,1)S(1)}, bf16[128,64]{0,1:T(8,128)(2,1)}, u32[]{:S(2)}) copy-start(bf16[128,64]{0,1:T(8,128)(2,1)} %param.20) | copy-start | bytes 49156
  7.2 186.2 %all-gather.3.cloned.1.call-start = ((), (), s32[]{:S(2)}) async-start(), calls=%async_computation.3 | async-start | bytes 1310720 | tf_op jit(solution)/shard_map/all_gather | solution.py:98
  10.4 1.3 copy-start.2
  13.0 19.3 %copy-start.13 = (bf16[256,128]{1,0:T(8,128)(2,1)S(1)}, bf16[256,128]{1,0:T(8,128)(2,1)}, u32[]{:S(2)}) copy-start(bf16[256,128]{1,0:T(8,128)(2,1)} %param.18) | copy-start | bytes 196612
  13.0 133.0 %collective-permute-start = (bf16[127,4096]{1,0:T(8,128)(2,1)}, bf16[127,4096]{1,0:T(8,128)(2,1)}, u32[]{:S(2)}, u32[]{:S(2)}) collective-permute-start(bf16[127,4096]{1,0:T(8,128)(2,1)} %slice.49), channel_id=1, source_target_pairs={{0,1},{1,2},{2,3},{3,4},{4,5},{5,6},{6,7},{7,8},{8,9},{9,10},{10,1... | collective-permute-start | bytes 3121160 | tf_op jit(solution)/shard_map/ppermute | solution.py:33
  20.6 165.9 %all-to-all-start = ((bf16[32,128,64]{1,2,0:T(8,128)(2,1)}), bf16[32,128,64]{1,2,0:T(8,128)(2,1)S(1)}, u32[]{:S(2)}, u32[]{:S(2)}) async-start(bf16[32,128,64]{1,2,0:T(8,128)(2,1)} %stack.2), calls=%async_computation | async-start | bytes 1048576 | tf_op jit(solution)/shard_map/all_to_all | solution.py:106
  28.5 353.3 %reduce-scatter.5.cloned.1.call-start = ((), (), s32[]{:S(2)}) async-start(), calls=%async_computation.6 | async-start | bytes 1310720 | tf_op jit(solution)/shard_map/reduce_scatter | solution.py:153
  157.3 3.3 copy-start.8
  180.8 5.6 copy-start.14
  186.4 5.5 copy-start.11
  193.4 756.4 %all-gather.5.cloned.1.call-start = ((), (), s32[]{:S(2)}) async-start(), calls=%async_computation.4 | async-start | bytes 34603008 | tf_op jit(solution)/shard_map/all_gather | solution.py:104
  194.1 951.1 %reduce-scatter.3.cloned.1.call-start = ((), (), s32[]{:S(2)}) async-start(), calls=%async_computation.5 | async-start | bytes 1081344 | tf_op jit(solution)/shard_map/reduce_scatter | solution.py:151
  301.1 56.8 %copy-start.15 = (bf16[64,1024]{1,0:T(8,128)(2,1)S(1)}, bf16[64,1024]{1,0:T(8,128)(2,1)}, u32[]{:S(2)}) copy-start(bf16[64,1024]{1,0:T(8,128)(2,1)} %param.21) | copy-start | bytes 393220
  949.8 17.2 %copy-start.3 = (bf16[256,4096]{1,0:T(8,128)(2,1)S(1)}, bf16[256,4096]{1,0:T(8,128)(2,1)}, u32[]{:S(2)}) copy-start(bf16[256,4096]{1,0:T(8,128)(2,1)} %copy-done.2) | copy-start | bytes 6291460
  949.8 17.2 %copy-start.9 = (f32[256,4096]{1,0:T(8,128)S(1)}, f32[256,4096]{1,0:T(8,128)}, u32[]{:S(2)}) copy-start(f32[256,4096]{1,0:T(8,128)} %copy.96) | copy-start | bytes 12582916
  949.8 17.2 %copy-start.10 = (bf16[1,256,4096]{2,1,0:T(8,128)(2,1)S(1)}, bf16[1,256,4096]{2,1,0:T(8,128)(2,1)}, u32[]{:S(2)}) copy-start(bf16[1,256,4096]{2,1,0:T(8,128)(2,1)} %param.11) | copy-start | bytes 6291460
  967.0 6.2 copy-start.18
  973.2 56.9 %copy-start.4 = (bf16[256,4096]{1,0:T(8,128)(2,1)}, bf16[256,4096]{1,0:T(8,128)(2,1)S(1)}, u32[]{:S(2)}) copy-start(bf16[256,4096]{1,0:T(8,128)(2,1)S(1)} %get-tuple-element.10) | copy-start | bytes 6291460
  998.2 60.7 %collective-permute-start.1 = (f32[127,4096]{1,0:T(8,128)}, f32[127,4096]{1,0:T(8,128)}, u32[]{:S(2)}, u32[]{:S(2)}) collective-permute-start(f32[127,4096]{1,0:T(8,128)} %copy.123), channel_id=1, source_target_pairs={{1,0},{2,1},{3,2},{4,3},{5,4},{6,5},{7,6},{8,7},{9,8},{10,9},{11,1... | collective-permute-start | bytes 6242312 | tf_op jit(solution)/shard_map/ppermute | solution.py:33
  1054.5 4.4 copy-start.5
  1054.5 4.4 copy-start.6
  1054.5 4.4 copy-start.7
  1059.0 124.3 %copy-start.1 = (bf16[1,256,4096]{2,1,0:T(8,128)(2,1)S(1)}, bf16[1,256,4096]{2,1,0:T(8,128)(2,1)}, u32[]{:S(2)}) copy-start(bf16[1,256,4096]{2,1,0:T(8,128)(2,1)} %param.14) | copy-start | bytes 6291460
Sparse Core Ops, SparseCore 0:
  19.7 28.5 all-gather.2
  193.5 33.8 reduce-scatter.4
  229.0 720.7 all-gather.4
  1002.9 142.2 reduce-scatter.2
